TPU v7x, 32 devices: a whole 2x2x4 slice. The times are simulated.
32 devices in a mesh: stream: 2 (over y), pairs: 16 (over z, x, core).
Axes of the slice: x: 2, y: 2, z: 4, core: 2. Of those that a mesh axis runs over, the one named last changes fastest.
Arguments:
- tokens: bfloat16 [2, 2, 8192, 768], P('stream', None, 'pairs'), may hold values from -6 to 6
- segments: int32 [2, 2, 16, 512], P('stream', None, 'pairs'), may hold values from 0 to 3, never falling along the last dimension, each value on 1 to 384 neighbouring positions
- counts: int32 [2, 16], replicated, may hold values from 2 to 4
- cotangent: bfloat16 [2, 2, 8192, 768], P('stream', None, 'pairs'), may hold values from -6 to 6
- w_query: bfloat16 [768, 768], replicated, may hold values from -0.21875 to 0.21875
- b_query: bfloat16 [768], replicated, may hold values from -3 to 3
- w_key: bfloat16 [768, 768], replicated, may hold values from -0.21875 to 0.21875
- w_value: bfloat16 [768, 768], replicated, may hold values from -0.21875 to 0.21875
- b_value: bfloat16 [768], replicated, may hold values from -3 to 3
- w_out: bfloat16 [768, 768], replicated, may hold values from -0.875 to 0.875
- b_out: bfloat16 [768], replicated, may hold values from -2 to 2
- gain_attn: bfloat16 [768], replicated, may hold values from 0.5 to 1.5
- bias_attn: bfloat16 [768], replicated, may hold values from -1.5 to 1.5
- w_inner: bfloat16 [768, 3072], replicated, may hold values from -0.21875 to 0.21875
- b_inner: bfloat16 [3072], replicated, may hold values from -3 to 3
- w_outer: bfloat16 [3072, 768], replicated, may hold values from -0.109375 to 0.109375
- b_outer: bfloat16 [768], replicated, may hold values from -2 to 2
- gain_ffn: bfloat16 [768], replicated, may hold values from 0.5 to 1.5
- bias_ffn: bfloat16 [768], replicated, may hold values from -0.796875 to 0.796875
Outputs:
- loss_rows: float32 [2, 2, 64], P('stream', None, 'pairs')
- embeddings: float32 [2, 2, 64, 768], P('stream', None, 'pairs')
- embedding_grads: float32 [2, 2, 64, 768], P('stream', None, 'pairs')
- hidden_states: bfloat16 [2, 2, 8192, 768], P('stream', None, 'pairs')
- token_grads: bfloat16 [2, 2, 8192, 768], P('stream', None, 'pairs')
- grad_w_query: float32 [768, 768], replicated
- grad_b_query: float32 [768], replicated
- grad_w_key: float32 [768, 768], replicated
- grad_w_value: float32 [768, 768], replicated
- grad_b_value: float32 [768], replicated
- grad_w_out: float32 [768, 768], replicated
- grad_b_out: float32 [768], replicated
- grad_gain_attn: float32 [768], replicated
- grad_bias_attn: float32 [768], replicated
- grad_w_inner: float32 [768, 3072], replicated
- grad_b_inner: float32 [3072], replicated
- grad_w_outer: float32 [3072, 768], replicated
- grad_b_outer: float32 [768], replicated
- grad_gain_ffn: float32 [768], replicated
- grad_bias_ffn: float32 [768], replicated
All inputs are finite; a program needn't handle non-finite values.
Results may differ from a plain program's by a relative error of at most 0.014.
Values sent between devices are 32-bit elements; how exact they have to be, the bound alone decides.
No kernel may reach another device: no remote copies, remote signals or barrier semaphores. Data moves between devices by JAX's collectives and lax.ppermute only.
A program may use at most 256 MiB of HBM per device.

v0:
```python
import jax
import jax.numpy as jnp
from jax import lax
from jax.sharding import PartitionSpec as P

D = 768
HEADS = 12
HEAD_DIM = 64
SLOTS = 4
HIGHEST = lax.Precision.HIGHEST
LOGIT_DIVISOR = 0.01
NORM_EPS = 1e-12
UNIT_EPS = 1e-06


def swapped(value, axis, apart):
    return lax.ppermute(value, axis, [(i, i ^ 1 << apart) for i in range(lax.axis_size(axis))])


def norm_forward(total, norm_gain, layer_offset):
    centered = total - jnp.mean(total, axis=-1, keepdims=True)
    inv_std = lax.rsqrt(jnp.mean(centered * centered, axis=-1, keepdims=True) + NORM_EPS)
    normed = centered * inv_std
    return (normed, inv_std, normed * norm_gain + layer_offset)


def norm_backward(upstream, normed, inv_std, norm_gain):
    through = upstream * norm_gain
    grad_total = inv_std * (
        through
        - jnp.mean(through, axis=-1, keepdims=True)
        - normed * jnp.mean(through * normed, axis=-1, keepdims=True)
    )
    return (grad_total, jnp.sum(upstream * normed, axis=0), jnp.sum(upstream, axis=0))


def unit_scale(pooled):
    return (
        pooled
        * lax.rsqrt(jnp.mean(pooled * pooled, axis=-1, keepdims=True) + UNIT_EPS)
        * D ** (-0.5)
    )


def exact_gelu(values_in):
    return jax.nn.gelu(values_in, approximate=False)


def on_device(
    tokens,
    segments,
    counts,
    cotangent,
    w_query,
    b_query,
    w_key,
    w_value,
    b_value,
    w_out,
    b_out,
    gain_attn,
    bias_attn,
    w_inner,
    b_inner,
    w_outer,
    b_outer,
    gain_ffn,
    bias_ffn,
):
    weights_all = (
        w_query,
        b_query,
        w_key,
        w_value,
        b_value,
        w_out,
        b_out,
        gain_attn,
        bias_attn,
        w_inner,
        b_inner,
        w_outer,
        b_outer,
        gain_ffn,
        bias_ffn,
    )
    sample_count = tokens.shape[1]
    length = tokens.shape[2]
    slots = SLOTS
    scale = HEAD_DIM ** (-0.5)
    pair_index = lax.axis_index("pairs")
    rows_all = slots * lax.axis_size("pairs")
    f32 = jnp.float32
    bf16 = jnp.bfloat16
    bias_query = b_query.astype(f32)
    bias_value = b_value.astype(f32)
    output_bias = b_out.astype(f32)
    gain_one = gain_attn.astype(f32)
    shift_one = bias_attn.astype(f32)
    bias_inner = b_inner.astype(f32)
    bias_outer = b_outer.astype(f32)
    gain_two = gain_ffn.astype(f32)
    shift_two = bias_ffn.astype(f32)
    column_ids = jnp.arange(rows_all, dtype=jnp.int32)
    slot_ids = jnp.arange(slots, dtype=jnp.int32)
    totals = [jnp.zeros(weight.shape, f32) for weight in weights_all]
    loss_list, unit_list, unit_grad_list, hidden_list, input_grad_list = ([], [], [], [], [])
    for batch_number in range(sample_count):
        inputs_low = tokens[0, batch_number]
        inputs_full = inputs_low.astype(f32)
        segment = segments[0, batch_number, 0]
        query_flat = (jnp.dot(inputs_low, w_query, preferred_element_type=f32) + bias_query).astype(
            bf16
        )
        key_flat = jnp.dot(inputs_low, w_key, preferred_element_type=f32).astype(bf16)
        value_flat = (jnp.dot(inputs_low, w_value, preferred_element_type=f32) + bias_value).astype(
            bf16
        )
        queries = query_flat.reshape(length, HEADS, HEAD_DIM)
        keys = key_flat.reshape(length, HEADS, HEAD_DIM)
        values = value_flat.reshape(length, HEADS, HEAD_DIM)
        same_segment = (segment[:, None] == segment[None, :])[None]

        def masked_scores():
            raw_scores = (
                jnp.einsum("qhd,khd->hqk", queries, keys, preferred_element_type=f32) * scale
            )
            return jnp.where(same_segment, raw_scores, -1000000000.0)

        scores = masked_scores()
        row_top = jnp.max(scores, axis=-1, keepdims=True)
        exponent = jnp.exp(scores - row_top)
        normalizer_total = jnp.sum(exponent, axis=-1, keepdims=True)
        log_total = row_top + jnp.log(normalizer_total)
        probs = (exponent / normalizer_total).astype(bf16)
        mixed = (
            jnp.einsum("hqk,khd->qhd", probs, values, preferred_element_type=f32)
            .astype(bf16)
            .reshape(length, D)
        )
        attended = jnp.dot(mixed, w_out, preferred_element_type=f32) + output_bias
        normed_one, inv_one, first = norm_forward(inputs_full + attended, gain_one, shift_one)
        first_low = first.astype(bf16)
        inner = jnp.dot(first_low, w_inner, preferred_element_type=f32) + bias_inner
        gelu_values, gelu_back = jax.vjp(exact_gelu, inner)
        activated = gelu_values.astype(bf16)
        outer = jnp.dot(activated, w_outer, preferred_element_type=f32) + bias_outer
        normed_two, inv_two, hidden = norm_forward(first + outer, gain_two, shift_two)
        hidden_list.append(hidden.astype(bf16))
        one_hot = (segment[None, :] == slot_ids[:, None]).astype(f32)
        counted = jnp.sum(one_hot, axis=1, keepdims=True)
        pooled = jnp.dot(one_hot, hidden, precision=HIGHEST, preferred_element_type=f32) / counted
        unit_rows, unit_back = jax.vjp(unit_scale, pooled)
        unit_list.append(unit_rows)
        partner_rows = swapped(unit_rows, "stream", 0)
        others = lax.all_gather(partner_rows, "pairs", axis=0, tiled=True)
        count_row = counts[batch_number]
        column_valid = column_ids % slots < jnp.repeat(
            count_row, slots, total_repeat_length=rows_all
        )
        own_count = lax.dynamic_index_in_dim(count_row, pair_index, keepdims=False)
        row_valid = (slot_ids < own_count).astype(f32)
        target = column_ids[None, :] == (pair_index * slots + slot_ids)[:, None]
        cosine_scores = (
            jnp.dot(unit_rows, others.T, precision=HIGHEST, preferred_element_type=f32)
            / LOGIT_DIVISOR
        )
        masked = jnp.where(column_valid[None, :], cosine_scores, -1000000000.0)
        log_sum = jax.nn.logsumexp(masked, axis=-1)
        diagonal = jnp.sum(jnp.where(target, cosine_scores, 0.0), axis=-1)
        loss_list.append((log_sum - diagonal) * row_valid)
        grad_logits = (
            (jnp.exp(masked - log_sum[:, None]) - target.astype(f32))
            * row_valid[:, None]
            / LOGIT_DIVISOR
        )
        own_grad = jnp.dot(grad_logits, others, precision=HIGHEST, preferred_element_type=f32)
        column_gradient = jnp.dot(
            grad_logits.T, unit_rows, precision=HIGHEST, preferred_element_type=f32
        )
        summed_back = lax.psum_scatter(column_gradient, "pairs", scatter_dimension=0, tiled=True)
        returned = swapped(summed_back, "stream", 0)
        unit_grad = own_grad + returned
        unit_grad_list.append(unit_grad)
        (pooled_grad,) = unit_back(unit_grad)
        grad_hidden = cotangent[0, batch_number].astype(f32) + jnp.dot(
            one_hot.T, pooled_grad / counted, precision=HIGHEST, preferred_element_type=f32
        )
        grad_second, grad_gain_two, grad_shift_two = norm_backward(
            grad_hidden, normed_two, inv_two, gain_two
        )
        second_low = grad_second.astype(bf16)
        grad_w_outer = jnp.einsum("tf,td->fd", activated, second_low, preferred_element_type=f32)
        grad_b_outer = jnp.sum(grad_second, axis=0)
        grad_act = jnp.einsum("td,fd->tf", second_low, w_outer, preferred_element_type=f32)
        (grad_inner,) = gelu_back(grad_act)
        inner_low = grad_inner.astype(bf16)
        grad_w_inner = jnp.einsum("td,tf->df", first_low, inner_low, preferred_element_type=f32)
        grad_b_inner = jnp.sum(grad_inner, axis=0)
        grad_first = grad_second + jnp.einsum(
            "tf,df->td", inner_low, w_inner, preferred_element_type=f32
        )
        grad_sum_one, grad_gain_one, grad_shift_one = norm_backward(
            grad_first, normed_one, inv_one, gain_one
        )
        attended_low = grad_sum_one.astype(bf16)
        grad_w_out = jnp.einsum("td,te->de", mixed, attended_low, preferred_element_type=f32)
        grad_mixed = (
            jnp.einsum("te,de->td", attended_low, w_out, preferred_element_type=f32)
            .astype(bf16)
            .reshape(length, HEADS, HEAD_DIM)
        )
        grad_probs = jnp.einsum("qhd,khd->hqk", grad_mixed, values, preferred_element_type=f32)
        grad_values = jnp.einsum(
            "hqk,qhd->khd", probs, grad_mixed, preferred_element_type=f32
        ).reshape(length, D)
        soft_again = jnp.exp(masked_scores() - log_total)
        grad_scores = (
            soft_again * (grad_probs - jnp.sum(soft_again * grad_probs, axis=-1, keepdims=True))
        ).astype(bf16)
        grad_queries = (
            jnp.einsum("hqk,khd->qhd", grad_scores, keys, preferred_element_type=f32) * scale
        ).reshape(length, D)
        grad_keys = (
            jnp.einsum("hqk,qhd->khd", grad_scores, queries, preferred_element_type=f32) * scale
        ).reshape(length, D)
        query_low = grad_queries.astype(bf16)
        key_low = grad_keys.astype(bf16)
        value_low = grad_values.astype(bf16)
        grad_w_query = jnp.einsum("td,te->de", inputs_low, query_low, preferred_element_type=f32)
        grad_w_key = jnp.einsum("td,te->de", inputs_low, key_low, preferred_element_type=f32)
        grad_w_value = jnp.einsum("td,te->de", inputs_low, value_low, preferred_element_type=f32)
        grad_b_query = jnp.sum(grad_queries, axis=0)
        grad_b_value = jnp.sum(grad_values, axis=0)
        grad_b_out = jnp.sum(grad_sum_one, axis=0)
        grad_input = grad_sum_one
        grad_input = grad_input + jnp.einsum(
            "te,de->td", query_low, w_query, preferred_element_type=f32
        )
        grad_input = grad_input + jnp.einsum(
            "te,de->td", key_low, w_key, preferred_element_type=f32
        )
        grad_input = grad_input + jnp.einsum(
            "te,de->td", value_low, w_value, preferred_element_type=f32
        )
        input_grad_list.append(grad_input.astype(bf16))
        batch_grads = (
            grad_w_query,
            grad_b_query,
            grad_w_key,
            grad_w_value,
            grad_b_value,
            grad_w_out,
            grad_b_out,
            grad_gain_one,
            grad_shift_one,
            grad_w_inner,
            grad_b_inner,
            grad_w_outer,
            grad_b_outer,
            grad_gain_two,
            grad_shift_two,
        )
        totals = [running + added for running, added in zip(totals, batch_grads)]
    totals = list(lax.psum(tuple(totals), ("stream", "pairs")))
    return (
        jnp.stack(loss_list)[None],
        jnp.stack(unit_list)[None],
        jnp.stack(unit_grad_list)[None],
        jnp.stack(hidden_list)[None],
        jnp.stack(input_grad_list)[None],
        totals[0],
        totals[1],
        totals[2],
        totals[3],
        totals[4],
        totals[5],
        totals[6],
        totals[7],
        totals[8],
        totals[9],
        totals[10],
        totals[11],
        totals[12],
        totals[13],
        totals[14],
    )


def solution(mesh):
    in_specs = (
        P("stream", None, "pairs", None),
        P("stream", None, "pairs", None),
        P(),
        P("stream", None, "pairs", None),
        P(),
        P(),
        P(),
        P(),
        P(),
        P(),
        P(),
        P(),
        P(),
        P(),
        P(),
        P(),
        P(),
        P(),
        P(),
    )
    out_specs = (
        P("stream", None, "pairs"),
        P("stream", None, "pairs", None),
        P("stream", None, "pairs", None),
        P("stream", None, "pairs", None),
        P("stream", None, "pairs", None),
        P(),
        P(),
        P(),
        P(),
        P(),
        P(),
        P(),
        P(),
        P(),
        P(),
        P(),
        P(),
        P(),
        P(),
        P(),
    )
    return jax.shard_map(
        on_device, mesh=mesh, in_specs=in_specs, out_specs=out_specs, check_vma=False
    )
```

profile of v0, /device:TPU:0, one launch (start us, length us, event | category | flops | bytes accessed | tf_op | source)
XLA Modules:
  0.0 890.0 jit_solution(1401948497027483996)
XLA Ops:
  10.3 3.2 add_convert_fusion.3
  26.6 2.6 copy.104
  29.2 2.3 copy.109
  31.5 2.3 copy.105
  33.8 2.3 copy.110
  36.1 2.3 copy.106
  38.4 3.5 fusion.2
  41.9 3.7 fusion
  46.6 4.3 divide_convert_fusion.1
  57.9 2.6 fusion.1
  62.5 3.4 divide_convert_fusion
  70.2 2.7 fusion.129
  73.0 34.6 %multiply_convert_fusion.3 = (bf16[512,3072]{1,0:T(8,128)(2,1)S(1)}, f32[512,3072]{1,0:T(8,128)}, bf16[512,3072]{1,0:T(8,128)(2,1)S(1)}, f32[512,3072]{1,0:T(8,128)}, f32[512,3072]{1,0:T(8,128)}) fusion(f32[3072]{0:T(1024)S(1)} %copy-done.89, f32[512,3072]{1,0:T(8,128)S(1)} %fusion.129, bf16[768,3072]{1,0:T(8,128)(2,1)S(1)} %bitcast.274, ...), kind=kOutput, calls=%fused_computation.37 | convolution fusion | flops 2625503232 | bytes 37771264 | tf_op jit(solution)/shard_map/dot_general | solution.py:144
  107.7 2.8 fusion.144
  112.5 3.0 collective-permute-start
  115.6 2.8 fusion.145
  128.3 22.6 %all-gather = f32[16,4,768]{2,1,0:T(4,128)S(1)} all-gather(f32[1,4,768]{2,1,0:T(4,128)S(1)} %bitcast.267), channel_id=1, replica_groups=mesh['stream'=2,'pairs'=16] {'pairs'}, dimensions={0}, use_global_device_ids=true | all-gather | bytes 208896 | tf_op jit(solution)/shard_map/all_gather | solution.py:156
  151.9 18.0 %all-gather.1 = f32[16,4,768]{2,1,0:T(4,128)S(1)} all-gather(f32[1,4,768]{2,1,0:T(4,128)S(1)} %bitcast.268), channel_id=1, replica_groups=mesh['stream'=2,'pairs'=16] {'pairs'}, dimensions={0}, use_global_device_ids=true | all-gather | bytes 208896 | tf_op jit(solution)/shard_map/all_gather | solution.py:156
  176.1 88.5 %all-reduce.10.cloned.1.call-done = (f32[64,768]{1,0:T(8,128)}, f32[64,768]{1,0:T(8,128)}) async-done(((f32[64,768]{1,0:T(8,128)}, f32[64,768]{1,0:T(8,128)}), (f32[64,768]{1,0:T(8,128)}, f32[64,768]{1,0:T(8,128)})) %all-reduce.10.cloned.1.call-update) | async-done | bytes 393232
  275.2 5.0 multiply_reduce_fusion.3
  280.3 2.9 fusion.134
  283.2 8.8 fusion.146
  292.0 7.2 multiply_reduce_fusion.5
  299.2 8.6 fusion.147
  307.8 8.6 fusion.137
  320.4 5.6 fusion.19
  326.0 5.2 fusion.74
  332.6 6.3 bitcast_convert_fusion.2
  339.0 10.3 %multiply_reduce_fusion.1 = (f32[12,512]{1,0:T(8,128)S(1)}, f32[12,512,512]{1,2,0:T(8,128)}) fusion(f32[12,512,512]{1,2,0:T(8,128)} %copy-done.2, f32[12,512]{1,0:T(8,128)S(1)} %copy-done.72, pred[512,512]{0,1:T(8,128)(4,1)S(1)} %copy-done.23, bf16[512,12,64]{0,2,1:T(8,128)(2,1)S(1)} %bitcast.234, bf16[512,12,64]{0,2,1:T(8,128)(2,1)S(1)} %bitcast.226), kind=kOutput, calls=%fused_computation.6 | convolution fusion | flops 418375680 | bytes 27049984 | tf_op jit(solution)/shard_map/qhd,khd->hqk/dot_general | solution.py:213
  349.3 7.2 multiply_convert_fusion.1
  356.5 3.0 multiply_convert_fusion.5
  359.5 2.6 bitcast_convert_fusion.3
  367.5 6.3 bitcast_convert_fusion
  373.9 10.3 %multiply_reduce_fusion = (f32[12,512]{1,0:T(8,128)S(1)}, f32[12,512,512]{1,2,0:T(8,128)}) fusion(f32[12,512,512]{1,2,0:T(8,128)} %copy-done.1, f32[12,512]{1,0:T(8,128)S(1)} %copy-done.73, pred[512,512]{0,1:T(8,128)(4,1)S(1)} %copy-done.22, bf16[512,12,64]{0,2,1:T(8,128)(2,1)S(1)} %bitcast.236, bf16[512,12,64]{0,2,1:T(8,128)(2,1)S(1)} %bitcast.224), kind=kOutput, calls=%fused_computation.3 | convolution fusion | flops 418375680 | bytes 27049984 | tf_op jit(solution)/shard_map/qhd,khd->hqk/dot_general | solution.py:213
  384.2 7.1 multiply_convert_fusion
  391.3 2.9 multiply_convert_fusion.4
  394.2 2.5 bitcast_convert_fusion.1
  397.1 2.2 convolution_add_fusion.2
  401.8 7.7 convolution_add_fusion.1
  409.5 7.1 convolution_add_fusion
  418.5 2.2 add_bitcast_fusion
  447.4 42.3 %all-reduce.2 = (f32[768]{0:T(1024)}, f32[768]{0:T(1024)}, f32[768]{0:T(1024)}, f32[768]{0:T(1024)}, f32[768]{0:T(1024)}, /*index=5*/f32[3072]{0:T(1024)}, f32[768]{0:T(1024)}, f32[768]{0:T(1024)}, f32[768]{0:T(1024)}) all-reduce(f32[768]{0:T(1024)} %add.434, ...), channel_id=1, replica_groups=mesh['stream'=2,'pairs'=16] {'stream','pairs'}, use_global_device_ids=true, to_apply=%region_39.41 | all-reduce | flops 9216 | bytes 73728 | tf_op jit(solution)/shard_map/psum | solution.py:265
  491.1 2.5 maximum_bitcast_fusion
  503.0 357.0 %all-reduce.8.cloned.1.call-done = (f32[768,768]{0,1:T(8,128)}, f32[768,768]{0,1:T(8,128)}, f32[768,768]{0,1:T(8,128)}, f32[768,768]{1,0:T(8,128)}, f32[768,3072]{1,0:T(8,128)}, /*index=5*/f32[3072,768]{1,0:T(8,128)}) async-done(((f32[768,768]{0,1:T(8,128)}, f32[768,768]{0,1:T(8,128)}, f32[768,768]{0,1:T(8,128)}, f32[768,768]{1,0:T(8,128)}, f32[768,3072]{1,0:T(8,128)}, /*index=5*/f32[3072,768]{1,0:T(8,128)}), ...) | async-done | bytes 28311568 | tf_op jit(solution)/shard_map/psum | solution.py:265
  860.0 3.2 copy.120
  865.1 3.2 copy.122
  869.7 9.3 %copy.140 = f32[768,3072]{1,0:T(8,128)} copy(f32[768,3072]{1,0:T(8,128)} %get-tuple-element.263) | data formatting | bytes 18874368
  879.1 3.7 copy.141
  (450 shorter events, 115.3 us)
Async XLA Ops:
  7.2 46.4 %copy-start = (bf16[768,768]{1,0:T(8,128)(2,1)S(1)}, bf16[768,768]{1,0:T(8,128)(2,1)}, u32[]{:S(2)}) copy-start(bf16[768,768]{1,0:T(8,128)(2,1)} %param.34) | copy-start | bytes 3538948
  7.2 257.4 %all-reduce.10.cloned.1.call-start = ((), (), s32[]{:S(2)}) async-start(), calls=%async_computation.1 | async-start | bytes 786432
  23.1 30.5 %copy-start.104 = (f32[768]{0:T(1024)}, f32[768]{0:T(1024)S(1)}, u32[]{:S(2)}) copy-start(f32[768]{0:T(1024)S(1)} %convert_element_type.218) | copy-start | bytes 9220
  26.6 39.3 %copy-start.13 = (bf16[512,768]{0,1:T(8,128)(2,1)}, bf16[512,768]{0,1:T(8,128)(2,1)S(1)}, u32[]{:S(2)}) copy-start(bf16[512,768]{0,1:T(8,128)(2,1)S(1)} %copy.108) | copy-start | bytes 2359300
  69.7 238.1 %copy-start.79 = (f32[512]{0:T(512)}, f32[512]{0:T(512)S(1)}, u32[]{:S(2)}) copy-start(f32[512]{0:T(512)S(1)} %broadcast_multiply_fusion.9) | copy-start | bytes 6148
  70.1 237.7 %copy-start.82 = (f32[512]{0:T(512)}, f32[512]{0:T(512)S(1)}, u32[]{:S(2)}) copy-start(f32[512]{0:T(512)S(1)} %add_rsqrt_fusion.1) | copy-start | bytes 6148
  70.2 37.4 %slice-start.15 = ((s8[4718592]{0:T(1024)(128)(4,1)}), s8[4194304]{0:T(1024)(128)(4,1)S(1)}, s32[]{:S(2)}) async-start(s8[4718592]{0:T(1024)(128)(4,1)} %bitcast.269), calls=%async_computation.17 | async-start | bytes 8388608
  73.0 34.6 %copy-start.130 = (f32[512,3072]{1,0:T(8,128)}, f32[512,3072]{1,0:T(8,128)S(1)}, u32[]{:S(2)}) copy-start(f32[512,3072]{1,0:T(8,128)S(1)} %fusion.129) | copy-start | bytes 18874372
  73.0 34.7 %copy-start.103 = (f32[768]{0:T(1024)S(1)}, f32[768]{0:T(1024)}, u32[]{:S(2)}) copy-start(f32[768]{0:T(1024)} %convert_element_type.224) | copy-start | bytes 9220
  73.0 34.6 %slice-start.16 = ((s8[4718592]{0:T(1024)(128)(4,1)}), s8[524288]{0:T(1024)(128)(4,1)S(1)}, s32[]{:S(2)}) async-start(s8[4718592]{0:T(1024)(128)(4,1)} %bitcast.269), calls=%async_computation.18 | async-start | bytes 1048576
  107.6 8.0 copy-start.31
  111.9 163.2 %copy-start.78 = (f32[4,768]{1,0:T(4,128)}, f32[4,768]{1,0:T(4,128)S(1)}, u32[]{:S(2)}) copy-start(f32[4,768]{1,0:T(4,128)S(1)} %get-tuple-element.209) | copy-start | bytes 36868
  112.5 15.8 %collective-permute-start = (f32[4,768]{1,0:T(4,128)S(1)}, f32[4,768]{1,0:T(4,128)S(1)}, u32[]{:S(2)}, u32[]{:S(2)}) collective-permute-start(f32[4,768]{1,0:T(4,128)S(1)} %multiply_multiply_fusion.11), channel_id=1, source_target_pairs={{0,16},{16,0},{1,17},{17,1},{2,18},{18,2},{3,19},{19,3},{4,20},{20... | collective-permute-start | bytes 36872 | tf_op jit(solution)/shard_map/ppermute | solution.py:17
  118.5 8.6 copy-start.129
  119.6 55.9 %copy-start.65 = (f32[12,512]{1,0:T(8,128)S(1)}, f32[12,512]{1,0:T(8,128)}, u32[]{:S(2)}) copy-start(f32[12,512]{1,0:T(8,128)} %copy-done.64) | copy-start | bytes 73732
  119.6 55.9 %copy-start.69 = (f32[12,512]{1,0:T(8,128)S(1)}, f32[12,512]{1,0:T(8,128)}, u32[]{:S(2)}) copy-start(f32[12,512]{1,0:T(8,128)} %copy-done.68) | copy-start | bytes 73732
  120.6 154.5 %copy-start.74 = (f32[4,768]{1,0:T(4,128)}, f32[4,768]{1,0:T(4,128)S(1)}, u32[]{:S(2)}) copy-start(f32[4,768]{1,0:T(4,128)S(1)} %get-tuple-element.215) | copy-start | bytes 36868
  121.2 30.7 %collective-permute-start.1 = (f32[4,768]{1,0:T(4,128)S(1)}, f32[4,768]{1,0:T(4,128)S(1)}, u32[]{:S(2)}, u32[]{:S(2)}) collective-permute-start(f32[4,768]{1,0:T(4,128)S(1)} %multiply_multiply_fusion.10), channel_id=1, source_target_pairs={{0,16},{16,0},{1,17},{17,1},{2,18},{18,2},{3,19},{19,3},{4,20},{20... | collective-permute-start | bytes 36872 | tf_op jit(solution)/shard_map/ppermute | solution.py:17
  125.9 44.0 %copy-start.92 = (pred[64]{0:T(512)(128)(4,1)}, pred[64]{0:T(512)(128)(4,1)S(1)}, u32[]{:S(2)}) copy-start(pred[64]{0:T(512)(128)(4,1)S(1)} %fusion.117) | copy-start | bytes 196
  151.4 115.6 %copy-start.98 = (f32[4]{0:T(128)}, f32[4]{0:T(128)S(1)}, u32[]{:S(2)}) copy-start(f32[4]{0:T(128)S(1)} %get-tuple-element.210) | copy-start | bytes 52
  170.3 96.6 %copy-start.100 = (f32[4]{0:T(128)}, f32[4]{0:T(128)S(1)}, u32[]{:S(2)}) copy-start(f32[4]{0:T(128)S(1)} %get-tuple-element.216) | copy-start | bytes 52
  171.8 92.8 %copy-start.102 = (f32[4]{0:T(128)}, f32[4]{0:T(128)S(1)}, u32[]{:S(2)}) copy-start(f32[4]{0:T(128)S(1)} %get-tuple-element.196) | copy-start | bytes 52
  171.8 95.2 %copy-start.101 = (f32[4]{0:T(128)}, f32[4]{0:T(128)S(1)}, u32[]{:S(2)}) copy-start(f32[4]{0:T(128)S(1)} %get-tuple-element.137) | copy-start | bytes 52
  175.4 684.6 %all-reduce.8.cloned.1.call-start = ((), (), s32[]{:S(2)}) async-start(), calls=%async_computation | async-start | bytes 56623104 | tf_op jit(solution)/shard_map/psum | solution.py:265
  264.6 10.5 %copy-start.45 = (f32[512,768]{1,0:T(8,128)S(1)}, f32[512,768]{1,0:T(8,128)}, u32[]{:S(2)}) copy-start(f32[512,768]{1,0:T(8,128)} %copy-done.44) | copy-start | bytes 4718596
  265.5 3.8 collective-permute-start.2
  267.7 3.7 collective-permute-start.3
  270.3 9.9 %copy-start.81 = (f32[4,768]{1,0:T(4,128)}, f32[4,768]{1,0:T(4,128)S(1)}, u32[]{:S(2)}) copy-start(f32[4,768]{1,0:T(4,128)S(1)} %get-tuple-element.219) | copy-start | bytes 36868
  275.2 8.0 slice-start.17
  283.2 24.6 %copy-start.41 = (f32[512,768]{1,0:T(8,128)}, f32[512,768]{1,0:T(8,128)S(1)}, u32[]{:S(2)}) copy-start(f32[512,768]{1,0:T(8,128)S(1)} %get-tuple-element.159) | copy-start | bytes 4718596
  283.2 8.8 copy-start.62
  283.2 8.8 copy-start.116
  307.8 8.7 copy-start.52
  332.6 16.6 %slice-start.3 = ((s8[12582912]{0:T(1024)(128)(4,1)}), s8[4194304]{0:T(1024)(128)(4,1)S(1)}, s32[]{:S(2)}) async-start(s8[12582912]{0:T(1024)(128)(4,1)} %bitcast.217), calls=%async_computation.5 | async-start | bytes 8388608
  339.0 10.3 %slice-start.4 = ((s8[12582912]{0:T(1024)(128)(4,1)}), s8[4194304]{0:T(1024)(128)(4,1)S(1)}, s32[]{:S(2)}) async-start(s8[12582912]{0:T(1024)(128)(4,1)} %bitcast.217), calls=%async_computation.6 | async-start | bytes 8388608
  339.0 10.3 %slice-start.5 = ((s8[12582912]{0:T(1024)(128)(4,1)}), s8[4194304]{0:T(1024)(128)(4,1)S(1)}, s32[]{:S(2)}) async-start(s8[12582912]{0:T(1024)(128)(4,1)} %bitcast.217), calls=%async_computation.7 | async-start | bytes 8388608
  367.5 16.7 %slice-start = ((s8[12582912]{0:T(1024)(128)(4,1)}), s8[4194304]{0:T(1024)(128)(4,1)S(1)}, s32[]{:S(2)}) async-start(s8[12582912]{0:T(1024)(128)(4,1)} %bitcast.215), calls=%async_computation.2 | async-start | bytes 8388608
  373.9 10.3 %slice-start.1 = ((s8[12582912]{0:T(1024)(128)(4,1)}), s8[4194304]{0:T(1024)(128)(4,1)S(1)}, s32[]{:S(2)}) async-start(s8[12582912]{0:T(1024)(128)(4,1)} %bitcast.215), calls=%async_computation.3 | async-start | bytes 8388608
  373.9 10.3 %slice-start.2 = ((s8[12582912]{0:T(1024)(128)(4,1)}), s8[4194304]{0:T(1024)(128)(4,1)S(1)}, s32[]{:S(2)}) async-start(s8[12582912]{0:T(1024)(128)(4,1)} %bitcast.215), calls=%async_computation.4 | async-start | bytes 8388608
  400.3 9.1 %slice-start.6 = ((s8[9437184]{0:T(1024)(128)(4,1)}), s8[4194304]{0:T(1024)(128)(4,1)S(1)}, s32[]{:S(2)}) async-start(s8[9437184]{0:T(1024)(128)(4,1)} %bitcast.219), calls=%async_computation.8 | async-start | bytes 8388608
  425.2 10.2 %copy-start.11 = (f32[12,64,512]{2,1,0:T(8,128)S(1)}, f32[12,64,512]{2,1,0:T(8,128)}, u32[]{:S(2)}) copy-start(f32[12,64,512]{2,1,0:T(8,128)} %get-tuple-element.236) | copy-start | bytes 4718596
  431.8 9.8 %copy-start.86 = (f32[768]{0:T(1024)S(1)}, f32[768]{0:T(1024)}, u32[]{:S(2)}) copy-start(f32[768]{0:T(1024)} %get-tuple-element.158) | copy-start | bytes 9220
  431.8 57.9 %copy-start.77 = (f32[4,768]{1,0:T(4,128)S(1)}, f32[4,768]{1,0:T(4,128)}, u32[]{:S(2)}) copy-start(f32[4,768]{1,0:T(4,128)} %copy-done.76) | copy-start | bytes 36868
  435.5 55.6 %copy-start.55 = (bf16[1,512,768]{2,1,0:T(8,128)(2,1)S(1)}, bf16[1,512,768]{2,1,0:T(8,128)(2,1)}, u32[]{:S(2)}) copy-start(bf16[1,512,768]{2,1,0:T(8,128)(2,1)} %get-tuple-element.171) | copy-start | bytes 2359300
  436.8 56.8 %copy-start.40 = (bf16[512,12,64]{0,2,1:T(8,128)(2,1)S(1)}, bf16[512,12,64]{0,2,1:T(8,128)(2,1)}, u32[]{:S(2)}) copy-start(bf16[512,12,64]{0,2,1:T(8,128)(2,1)} %get-tuple-element.235) | copy-start | bytes 2359300
  868.3 10.7 %slice-start.12 = ((s8[9437184]{0:T(1024)(128)(4,1)}), s8[4194304]{0:T(1024)(128)(4,1)S(1)}, s32[]{:S(2)}) async-start(s8[9437184]{0:T(1024)(128)(4,1)} %bitcast.231), calls=%async_computation.14 | async-start | bytes 8388608
  869.7 9.3 %slice-start.13 = ((s8[9437184]{0:T(1024)(128)(4,1)}), s8[4194304]{0:T(1024)(128)(4,1)S(1)}, s32[]{:S(2)}) async-start(s8[9437184]{0:T(1024)(128)(4,1)} %bitcast.231), calls=%async_computation.15 | async-start | bytes 8388608
  869.7 9.3 %slice-start.14 = ((s8[9437184]{0:T(1024)(128)(4,1)}), s8[1048576]{0:T(1024)(128)(4,1)S(1)}, s32[]{:S(2)}) async-start(s8[9437184]{0:T(1024)(128)(4,1)} %bitcast.231), calls=%async_computation.16 | async-start | bytes 2097152
  (112 other events, 396.8 us)
Sparse Core Ops, SparseCore 0:
  175.5 89.0 all-reduce.9
  425.3 434.6 all-reduce.7
where the time goes:
time: 900 us; the launch traced here: 890 us
  waiting for transfers between devices  447 us (50%)
  matrix products  204 us (23%)
  blocking collectives  82.9 us (9%)
  other arithmetic  70.3 us (8%)
  local copies, waits for them, and re-layouts  64 us (7%)
  between operations  16.7 us (2%)
    psum x1, waiting for transfers between devices, on_device(): totals = list(lax.psum(tuple(totals), ('stream', 'pairs')))  357 us
    unnamed x3, waiting for transfers between devices  88.6 us
    psum x1, blocking collectives, on_device(): totals = list(lax.psum(tuple(totals), ('stream', 'pairs')))  42.3 us
    unnamed x319, local copies, waits for them, and re-layouts  41.6 us
    all_gather x2, blocking collectives, on_device(): others = lax.all_gather(partner_rows, 'pairs', axis=0, tiled=True)  40.6 us
    dot_general x2, matrix products, on_device(): inner = jnp.dot(first_low, w_inner, preferred_element_type=f32) + bias_inner  37.3 us
    dot_general x2, matrix products, on_device(): jnp.einsum('qhd,khd->hqk', grad_mixed, values, preferred_element_type=f32)  20.5 us
  transfers between devices with their start and end apart: 6, of which 4 were waited for; matrix products, arithmetic and copies ran while one was open for 5% of the time, Pallas kernels for 0%

commit v1 on v0

--- a/solution.py
+++ b/solution.py
@@ -262,7 +262,7 @@
             grad_shift_two,
         )
         totals = [running + added for running, added in zip(totals, batch_grads)]
-    totals = list(lax.psum(tuple(totals), ("stream", "pairs")))
+    totals = list(lax.psum(lax.psum(tuple(totals), "pairs"), "stream"))
     return (
         jnp.stack(loss_list)[None],
         jnp.stack(unit_list)[None],

time: 900 us -> 1590 us (1.77)
  waiting for transfers between devices: 447 us -> 1110 us
  blocking collectives: 82.9 us -> 114 us
    psum x1 -> x2, waiting for transfers between devices: 357 us -> 1020 us  [on_device(): totals = list(lax.psum(lax.psum(tuple(totals), 'pairs'), 'stream'))]
    psum x1 -> x2, blocking collectives: 42.3 us -> 73.2 us  [on_device(): totals = list(lax.psum(lax.psum(tuple(totals), 'pairs'), 'stream'))]
    unnamed x3 -> x4, waiting for transfers between devices: 88.6 us -> 88.6 us
  transfers between devices with their start and end apart: 6 -> 7, of which waited for: 4 -> 5; matrix products, arithmetic and copies ran while one was open for 5% -> 3% of each run, Pallas kernels for 0% -> 0%
where the time goes in v1:
time: 1590 us; the launch traced here: 1580 us
  waiting for transfers between devices  1110 us (70%)
  matrix products  204 us (13%)
  blocking collectives  114 us (7%)
  other arithmetic  70.1 us (4%)
  local copies, waits for them, and re-layouts  64 us (4%)
  between operations  16.5 us (1%)
    psum x2, waiting for transfers between devices, on_device(): totals = list(lax.psum(lax.psum(tuple(totals), 'pairs'), 'stream'))  1020 us
    unnamed x4, waiting for transfers between devices  88.6 us
    psum x2, blocking collectives, on_device(): totals = list(lax.psum(lax.psum(tuple(totals), 'pairs'), 'stream'))  73.2 us
    unnamed x319, local copies, waits for them, and re-layouts  41.7 us
    all_gather x2, blocking collectives, on_device(): others = lax.all_gather(partner_rows, 'pairs', axis=0, tiled=True)  40.6 us
    dot_general x2, matrix products, on_device(): inner = jnp.dot(first_low, w_inner, preferred_element_type=f32) + bias_inner  37.3 us
  transfers between devices with their start and end apart: 7, of which 5 were waited for; matrix products, arithmetic and copies ran while one was open for 3% of the time, Pallas kernels for 0%

profile of v1, /device:TPU:0, one launch (start us, length us, event | category | flops | bytes accessed | tf_op | source)
XLA Modules:
  0.0 1579.6 jit_solution(3022894525749933704)
XLA Ops:
  10.3 3.2 add_convert_fusion.3
  26.6 2.6 copy.104
  29.2 2.3 copy.109
  31.5 2.3 copy.105
  33.9 2.3 copy.110
  36.1 2.3 copy.106
  38.5 3.5 fusion.2
  42.0 3.7 fusion
  46.7 4.3 divide_convert_fusion.1
  58.0 2.6 fusion.1
  62.5 3.4 divide_convert_fusion
  70.2 2.7 fusion.129
  73.1 34.6 %multiply_convert_fusion.3 = (bf16[512,3072]{1,0:T(8,128)(2,1)S(1)}, f32[512,3072]{1,0:T(8,128)}, bf16[512,3072]{1,0:T(8,128)(2,1)S(1)}, f32[512,3072]{1,0:T(8,128)}, f32[512,3072]{1,0:T(8,128)}) fusion(f32[3072]{0:T(1024)S(1)} %copy-done.89, f32[512,3072]{1,0:T(8,128)S(1)} %fusion.129, bf16[768,3072]{1,0:T(8,128)(2,1)S(1)} %bitcast.274, ...), kind=kOutput, calls=%fused_computation.37 | convolution fusion | flops 2625503232 | bytes 37771264 | tf_op jit(solution)/shard_map/dot_general | solution.py:144
  107.8 2.8 fusion.144
  112.5 3.0 collective-permute-start
  115.6 2.8 fusion.145
  128.3 22.6 %all-gather = f32[16,4,768]{2,1,0:T(4,128)S(1)} all-gather(f32[1,4,768]{2,1,0:T(4,128)S(1)} %bitcast.267), channel_id=1, replica_groups=mesh['stream'=2,'pairs'=16] {'pairs'}, dimensions={0}, use_global_device_ids=true | all-gather | bytes 208896 | tf_op jit(solution)/shard_map/all_gather | solution.py:156
  151.9 18.0 %all-gather.1 = f32[16,4,768]{2,1,0:T(4,128)S(1)} all-gather(f32[1,4,768]{2,1,0:T(4,128)S(1)} %bitcast.268), channel_id=1, replica_groups=mesh['stream'=2,'pairs'=16] {'pairs'}, dimensions={0}, use_global_device_ids=true | all-gather | bytes 208896 | tf_op jit(solution)/shard_map/all_gather | solution.py:156
  176.1 88.5 %all-reduce.13.cloned.1.call-done = (f32[64,768]{1,0:T(8,128)}, f32[64,768]{1,0:T(8,128)}) async-done(((f32[64,768]{1,0:T(8,128)}, f32[64,768]{1,0:T(8,128)}), (f32[64,768]{1,0:T(8,128)}, f32[64,768]{1,0:T(8,128)})) %all-reduce.13.cloned.1.call-update) | async-done | bytes 393232
  275.2 5.0 multiply_reduce_fusion.3
  280.3 2.9 fusion.134
  283.2 8.8 fusion.146
  292.0 7.2 multiply_reduce_fusion.5
  299.2 8.6 fusion.147
  307.8 8.6 fusion.137
  320.4 5.6 fusion.19
  326.0 5.2 fusion.74
  332.6 6.3 bitcast_convert_fusion.2
  339.0 10.3 multiply_reduce_fusion.1
  349.3 7.2 multiply_convert_fusion.1
  356.5 2.9 multiply_convert_fusion.5
  359.5 2.5 bitcast_convert_fusion.3
  367.5 6.3 bitcast_convert_fusion
  373.9 10.3 multiply_reduce_fusion
  384.2 7.1 multiply_convert_fusion
  391.3 2.9 multiply_convert_fusion.4
  394.2 2.6 bitcast_convert_fusion.1
  401.8 7.7 convolution_add_fusion.1
  409.5 7.1 convolution_add_fusion
  425.2 488.2 %all-reduce.11.cloned.1.call-done = (f32[768,768]{0,1:T(8,128)}, f32[768,768]{0,1:T(8,128)}, f32[768,768]{0,1:T(8,128)}, f32[768,768]{1,0:T(8,128)}, f32[768,3072]{1,0:T(8,128)}, /*index=5*/f32[3072,768]{1,0:T(8,128)}) async-done(((f32[768,768]{0,1:T(8,128)}, f32[768,768]{0,1:T(8,128)}, f32[768,768]{0,1:T(8,128)}, f32[768,768]{1,0:T(8,128)}, f32[768,3072]{1,0:T(8,128)}, /*index=5*/f32[3072,768]{1,0:T(8,128)}), ...) | async-done | bytes 28311568 | tf_op jit(solution)/shard_map/psum | solution.py:265
  935.5 62.1 %all-reduce.2 = (f32[768]{0:T(1024)}, f32[768]{0:T(1024)}, f32[768]{0:T(1024)}, f32[768]{0:T(1024)}, f32[768]{0:T(1024)}, /*index=5*/f32[3072]{0:T(1024)}, f32[768]{0:T(1024)}, f32[768]{0:T(1024)}, f32[768]{0:T(1024)}) all-reduce(f32[768]{0:T(1024)} %add.464, f32[768]{0:T(1024)} %add.470, ...), channel_id=1, replica_groups=mesh['stream'=2,'pairs'=16] {'pairs'}, use_global_device_ids=true, to_apply=%region_40.42 | all-reduce | flops 9216 | bytes 73728 | tf_op jit(solution)/shard_map/psum | solution.py:265
  997.7 11.1 all-reduce.5
  1010.2 2.4 maximum_bitcast_fusion
  1022.1 527.7 %all-reduce.15.cloned.1.call-done = (f32[768,768]{0,1:T(8,128)}, f32[768,768]{0,1:T(8,128)}, f32[768,768]{0,1:T(8,128)}, f32[768,768]{1,0:T(8,128)}, f32[768,3072]{1,0:T(8,128)}, /*index=5*/f32[3072,768]{1,0:T(8,128)}) async-done(((f32[768,768]{0,1:T(8,128)}, f32[768,768]{0,1:T(8,128)}, f32[768,768]{0,1:T(8,128)}, f32[768,768]{1,0:T(8,128)}, f32[768,3072]{1,0:T(8,128)}, /*index=5*/f32[3072,768]{1,0:T(8,128)}), ...) | async-done | bytes 28311568 | tf_op jit(solution)/shard_map/psum | solution.py:265
  1549.8 3.2 copy.120
  1554.9 3.2 copy.122
  1559.6 9.3 copy.146
  1568.9 3.7 copy.147
  (454 shorter events, 119.6 us)
Async XLA Ops:
  7.2 46.5 %copy-start = (bf16[768,768]{1,0:T(8,128)(2,1)S(1)}, bf16[768,768]{1,0:T(8,128)(2,1)}, u32[]{:S(2)}) copy-start(bf16[768,768]{1,0:T(8,128)(2,1)} %param.34) | copy-start | bytes 3538948
  7.2 257.4 %all-reduce.13.cloned.1.call-start = ((), (), s32[]{:S(2)}) async-start(), calls=%async_computation.1 | async-start | bytes 786432
  23.1 30.6 %copy-start.104 = (f32[768]{0:T(1024)}, f32[768]{0:T(1024)S(1)}, u32[]{:S(2)}) copy-start(f32[768]{0:T(1024)S(1)} %convert_element_type.218) | copy-start | bytes 9220
  26.6 39.4 %copy-start.13 = (bf16[512,768]{0,1:T(8,128)(2,1)}, bf16[512,768]{0,1:T(8,128)(2,1)S(1)}, u32[]{:S(2)}) copy-start(bf16[512,768]{0,1:T(8,128)(2,1)S(1)} %copy.108) | copy-start | bytes 2359300
  69.8 238.0 %copy-start.79 = (f32[512]{0:T(512)}, f32[512]{0:T(512)S(1)}, u32[]{:S(2)}) copy-start(f32[512]{0:T(512)S(1)} %broadcast_multiply_fusion.9) | copy-start | bytes 6148
  70.2 237.6 %copy-start.82 = (f32[512]{0:T(512)}, f32[512]{0:T(512)S(1)}, u32[]{:S(2)}) copy-start(f32[512]{0:T(512)S(1)} %add_rsqrt_fusion.1) | copy-start | bytes 6148
  70.2 37.4 %slice-start.15 = ((s8[4718592]{0:T(1024)(128)(4,1)}), s8[4194304]{0:T(1024)(128)(4,1)S(1)}, s32[]{:S(2)}) async-start(s8[4718592]{0:T(1024)(128)(4,1)} %bitcast.269), calls=%async_computation.18 | async-start | bytes 8388608
  73.0 34.6 %copy-start.130 = (f32[512,3072]{1,0:T(8,128)}, f32[512,3072]{1,0:T(8,128)S(1)}, u32[]{:S(2)}) copy-start(f32[512,3072]{1,0:T(8,128)S(1)} %fusion.129) | copy-start | bytes 18874372
  73.0 34.6 %copy-start.103 = (f32[768]{0:T(1024)S(1)}, f32[768]{0:T(1024)}, u32[]{:S(2)}) copy-start(f32[768]{0:T(1024)} %convert_element_type.224) | copy-start | bytes 9220
  73.0 34.6 %slice-start.16 = ((s8[4718592]{0:T(1024)(128)(4,1)}), s8[524288]{0:T(1024)(128)(4,1)S(1)}, s32[]{:S(2)}) async-start(s8[4718592]{0:T(1024)(128)(4,1)} %bitcast.269), calls=%async_computation.19 | async-start | bytes 1048576
  112.0 163.2 %copy-start.78 = (f32[4,768]{1,0:T(4,128)}, f32[4,768]{1,0:T(4,128)S(1)}, u32[]{:S(2)}) copy-start(f32[4,768]{1,0:T(4,128)S(1)} %get-tuple-element.224) | copy-start | bytes 36868
  112.5 15.8 collective-permute-start
  118.5 8.5 copy-start.129
  119.6 55.8 %copy-start.65 = (f32[12,512]{1,0:T(8,128)S(1)}, f32[12,512]{1,0:T(8,128)}, u32[]{:S(2)}) copy-start(f32[12,512]{1,0:T(8,128)} %copy-done.64) | copy-start | bytes 73732
  119.6 55.9 %copy-start.69 = (f32[12,512]{1,0:T(8,128)S(1)}, f32[12,512]{1,0:T(8,128)}, u32[]{:S(2)}) copy-start(f32[12,512]{1,0:T(8,128)} %copy-done.68) | copy-start | bytes 73732
  120.6 154.5 %copy-start.74 = (f32[4,768]{1,0:T(4,128)}, f32[4,768]{1,0:T(4,128)S(1)}, u32[]{:S(2)}) copy-start(f32[4,768]{1,0:T(4,128)S(1)} %get-tuple-element.230) | copy-start | bytes 36868
  121.2 30.7 %collective-permute-start.1 = (f32[4,768]{1,0:T(4,128)S(1)}, f32[4,768]{1,0:T(4,128)S(1)}, u32[]{:S(2)}, u32[]{:S(2)}) collective-permute-start(f32[4,768]{1,0:T(4,128)S(1)} %multiply_multiply_fusion.10), channel_id=1, source_target_pairs={{0,16},{16,0},{1,17},{17,1},{2,18},{18,2},{3,19},{19,3},{4,20},{20... | collective-permute-start | bytes 36872 | tf_op jit(solution)/shard_map/ppermute | solution.py:17
  125.9 43.9 %copy-start.92 = (pred[64]{0:T(512)(128)(4,1)}, pred[64]{0:T(512)(128)(4,1)S(1)}, u32[]{:S(2)}) copy-start(pred[64]{0:T(512)(128)(4,1)S(1)} %fusion.117) | copy-start | bytes 196
  151.4 115.6 %copy-start.98 = (f32[4]{0:T(128)}, f32[4]{0:T(128)S(1)}, u32[]{:S(2)}) copy-start(f32[4]{0:T(128)S(1)} %get-tuple-element.225) | copy-start | bytes 52
  170.3 96.7 %copy-start.100 = (f32[4]{0:T(128)}, f32[4]{0:T(128)S(1)}, u32[]{:S(2)}) copy-start(f32[4]{0:T(128)S(1)} %get-tuple-element.231) | copy-start | bytes 52
  171.8 92.8 %copy-start.102 = (f32[4]{0:T(128)}, f32[4]{0:T(128)S(1)}, u32[]{:S(2)}) copy-start(f32[4]{0:T(128)S(1)} %get-tuple-element.211) | copy-start | bytes 52
  171.8 95.2 %copy-start.101 = (f32[4]{0:T(128)}, f32[4]{0:T(128)S(1)}, u32[]{:S(2)}) copy-start(f32[4]{0:T(128)S(1)} %get-tuple-element.137) | copy-start | bytes 52
  175.4 738.1 %all-reduce.11.cloned.1.call-start = ((), (), s32[]{:S(2)}) async-start(), calls=%async_computation | async-start | bytes 56623104 | tf_op jit(solution)/shard_map/psum | solution.py:265
  264.6 10.5 copy-start.45
  265.5 3.8 collective-permute-start.2
  267.7 3.7 collective-permute-start.3
  270.3 9.9 copy-start.81
  275.2 8.0 slice-start.17
  283.2 24.6 %copy-start.41 = (f32[512,768]{1,0:T(8,128)}, f32[512,768]{1,0:T(8,128)S(1)}, u32[]{:S(2)}) copy-start(f32[512,768]{1,0:T(8,128)S(1)} %get-tuple-element.174) | copy-start | bytes 4718596
  283.2 8.8 copy-start.62
  283.2 8.8 copy-start.116
  307.8 8.6 copy-start.52
  332.6 16.7 %slice-start.3 = ((s8[12582912]{0:T(1024)(128)(4,1)}), s8[4194304]{0:T(1024)(128)(4,1)S(1)}, s32[]{:S(2)}) async-start(s8[12582912]{0:T(1024)(128)(4,1)} %bitcast.217), calls=%async_computation.6 | async-start | bytes 8388608
  339.0 10.3 slice-start.4
  339.0 10.3 slice-start.5
  367.5 16.7 %slice-start = ((s8[12582912]{0:T(1024)(128)(4,1)}), s8[4194304]{0:T(1024)(128)(4,1)S(1)}, s32[]{:S(2)}) async-start(s8[12582912]{0:T(1024)(128)(4,1)} %bitcast.215), calls=%async_computation.3 | async-start | bytes 8388608
  373.9 10.3 slice-start.1
  373.9 10.3 slice-start.2
  400.4 9.1 slice-start.6
  425.2 1124.6 %all-reduce.15.cloned.1.call-start = ((), (), s32[]{:S(2)}) async-start(), calls=%async_computation.2 | async-start | bytes 56623104 | tf_op jit(solution)/shard_map/psum | solution.py:265
  913.5 10.0 copy-start.11
  919.9 9.8 copy-start.86
  919.9 88.8 %copy-start.77 = (f32[4,768]{1,0:T(4,128)S(1)}, f32[4,768]{1,0:T(4,128)}, u32[]{:S(2)}) copy-start(f32[4,768]{1,0:T(4,128)} %copy-done.76) | copy-start | bytes 36868
  923.7 86.5 %copy-start.55 = (bf16[1,512,768]{2,1,0:T(8,128)(2,1)S(1)}, bf16[1,512,768]{2,1,0:T(8,128)(2,1)}, u32[]{:S(2)}) copy-start(bf16[1,512,768]{2,1,0:T(8,128)(2,1)} %get-tuple-element.186) | copy-start | bytes 2359300
  924.9 87.7 %copy-start.40 = (bf16[512,12,64]{0,2,1:T(8,128)(2,1)S(1)}, bf16[512,12,64]{0,2,1:T(8,128)(2,1)}, u32[]{:S(2)}) copy-start(bf16[512,12,64]{0,2,1:T(8,128)(2,1)} %get-tuple-element.250) | copy-start | bytes 2359300
  1558.1 10.7 slice-start.12
  1559.6 9.3 slice-start.13
  1559.6 9.3 slice-start.14
  (113 other events, 404.6 us)
Sparse Core Ops, SparseCore 0:
  175.5 89.0 all-reduce.12
  425.3 488.1 all-reduce.10
  916.4 633.3 all-reduce.14
